TPU v7x, 128 devices: a whole 4x4x4 slice. The times are simulated.
128 devices in a mesh: row: 16 (over y, z), col: 8 (over x, core).
Axes of the slice: x: 4, y: 4, z: 4, core: 2. Of those that a mesh axis runs over, the one named last changes fastest.
Arguments:
- voltages: float32 [4, 1, 2, 16384], P(None, None, None, ('row', 'col')), may hold values from -6 to 6
- antenna_gains: float32 [2, 16384], P(None, ('row', 'col')), may hold values from -5 to 5
- receiving_tile_index: int32 [4, 16384, 1], P(None, ('row', 'col')), may hold values from 0 to 127; in each aligned block of 128 rows (0 to 127, 128 to 255, ..., all dimensions but the last counted through in order) at most 3 rows name the same one
- cell_index: int32 [4, 16384], P(None, ('row', 'col')), may hold values from 0 to 131071
- beam_weights: float32 [4, 4096, 4096], P(None, ('row', 'col')), may hold values from 0.5 to 2000, as said below
Outputs:
- gain_gradient: float32 [2, 16384], P(None, ('row', 'col'))
Inputs may be any that keep to these rules, and one draw needn't show every extreme that they name: `receiving_tile_index`: tile t covers grid rows from (t // 8) * 256 and columns from (t % 8) * 512; among the 128 antennas of one device in one channel at most 3 name the same tile. `cell_index`: the cell's row within the tile is cell // 512, its column cell % 512. `beam_weights`: positive weights.
All inputs are finite; a program needn't handle non-finite values.
Results may differ from a plain program's by a relative error of at most 0.0003.
Values sent between devices are 32-bit elements; how exact they have to be, the bound alone decides.
No kernel may reach another device: no remote copies, remote signals or barrier semaphores. Data moves between devices by JAX's collectives and lax.ppermute only.
A program may use at most 64 MiB of HBM per device.

v0:
```python
import math

import jax
import jax.numpy as jnp
from jax import lax
from jax.sharding import PartitionSpec as P

GRID_SIDE = 4096


highest = lax.Precision.HIGHEST


def phase_table(height, across, period, direction):
    product = (
        jnp.arange(height, dtype=jnp.int32)[:, None]
        * jnp.arange(across, dtype=jnp.int32)[None, :]
        % period
    )
    angles = product.astype(jnp.float32) * (direction * 2.0 * math.pi / period)
    return (jnp.cos(angles), jnp.sin(angles))


def complex_einsum(pattern, factor, phases):
    real_part = jnp.einsum(pattern, factor[0], phases[0], precision=highest) - jnp.einsum(
        pattern, factor[1], phases[1], precision=highest
    )
    imag_part = jnp.einsum(pattern, factor[0], phases[1], precision=highest) + jnp.einsum(
        pattern, factor[1], phases[0], precision=highest
    )
    return (real_part, imag_part)


def complex_scale(values, phases):
    return (
        values[0] * phases[0] - values[1] * phases[1],
        values[0] * phases[1] + values[1] * phases[0],
    )


def mesh_sizes():
    row_count = lax.axis_size("row")
    col_count = lax.axis_size("col")
    return (row_count, col_count, row_count * col_count)


def rows_forward(blocks):
    frame_count = blocks.shape[0]
    row_count, col_count, device_count = mesh_sizes()
    inner_length = 128
    tile_cols = GRID_SIDE // col_count
    slab_rows = GRID_SIDE // device_count
    groups = tile_cols // inner_length
    outer_len = GRID_SIDE // inner_length
    shaped = blocks.reshape(frame_count, 2, col_count, slab_rows, groups, inner_length)
    first_phases = tuple(
        (
            member.reshape(outer_len, col_count, groups)
            for member in phase_table(outer_len, outer_len, outer_len, -1.0)
        )
    )
    middle = complex_einsum("fbpmn,kbm->fpkn", (shaped[:, 0], shaped[:, 1]), first_phases)
    middle = complex_scale(middle, phase_table(outer_len, inner_length, GRID_SIDE, -1.0))
    result = complex_einsum(
        "fpkn,jn->fjpk", middle, phase_table(inner_length, inner_length, inner_length, -1.0)
    )
    return jnp.stack(result, 1).reshape(frame_count, 2, inner_length, slab_rows * outer_len)


def rows_adjoint(blocks):
    frame_count = blocks.shape[0]
    row_count, col_count, device_count = mesh_sizes()
    inner_length = 128
    tile_cols = GRID_SIDE // col_count
    slab_rows = GRID_SIDE // device_count
    groups = tile_cols // inner_length
    outer_len = GRID_SIDE // inner_length
    shaped = blocks.reshape(frame_count, 2, inner_length, slab_rows, outer_len)
    middle = complex_einsum(
        "fjpk,jn->fpkn",
        (shaped[:, 0], shaped[:, 1]),
        phase_table(inner_length, inner_length, inner_length, 1.0),
    )
    middle = complex_scale(middle, phase_table(outer_len, inner_length, GRID_SIDE, 1.0))
    first_phases = tuple(
        (
            member.reshape(outer_len, col_count, groups)
            for member in phase_table(outer_len, outer_len, outer_len, 1.0)
        )
    )
    result = complex_einsum("fpkn,kbm->fbpmn", middle, first_phases)
    return jnp.stack(result, 1).reshape(frame_count, 2, col_count, slab_rows * tile_cols)


def columns_forward(blocks):
    frame_count = blocks.shape[0]
    row_count, col_count, device_count = mesh_sizes()
    inner_length = 128
    per_device = inner_length // device_count
    slab_rows = GRID_SIDE // device_count
    outer_len = GRID_SIDE // inner_length
    shaped = blocks.reshape(frame_count, 2, device_count, per_device, slab_rows, outer_len)
    middle = complex_einsum(
        "fskpa,us->fkpau",
        (shaped[:, 0], shaped[:, 1]),
        phase_table(device_count, device_count, device_count, -1.0),
    )
    twiddles = phase_table(slab_rows, device_count, GRID_SIDE, -1.0)
    middle = complex_scale(middle, (twiddles[0][:, None, :], twiddles[1][:, None, :]))
    result = complex_einsum(
        "fkpau,vp->fkavu", middle, phase_table(slab_rows, slab_rows, slab_rows, -1.0)
    )
    return jnp.stack(result, 1).reshape(
        frame_count, 2, per_device * outer_len, slab_rows * device_count
    )


def columns_adjoint(spectrum):
    frame_count = spectrum.shape[0]
    row_count, col_count, device_count = mesh_sizes()
    inner_length = 128
    per_device = inner_length // device_count
    slab_rows = GRID_SIDE // device_count
    outer_len = GRID_SIDE // inner_length
    shaped = spectrum.reshape(frame_count, 2, per_device, outer_len, slab_rows, device_count)
    middle = complex_einsum(
        "fkavu,vp->fkpau",
        (shaped[:, 0], shaped[:, 1]),
        phase_table(slab_rows, slab_rows, slab_rows, 1.0),
    )
    twiddles = phase_table(slab_rows, device_count, GRID_SIDE, 1.0)
    middle = complex_scale(middle, (twiddles[0][:, None, :], twiddles[1][:, None, :]))
    result = complex_einsum(
        "fkpau,us->fskpa", middle, phase_table(device_count, device_count, device_count, 1.0)
    )
    return jnp.stack(result, 1).reshape(frame_count, 2, inner_length, slab_rows * outer_len)


def keep_blocks(blocks):
    return blocks


def column_move(blocks, local_work):
    return local_work(lax.all_to_all(blocks, "col", split_axis=2, concat_axis=2, tiled=True))


def spectrum_move(blocks, local_work):
    result = local_work(
        lax.all_to_all(blocks, ("row", "col"), split_axis=2, concat_axis=2, tiled=True)
    )
    return result


def route_out(values, cell_ids):
    result = (
        lax.all_to_all(values, ("row", "col"), split_axis=1, concat_axis=1, tiled=True),
        lax.all_to_all(cell_ids, ("row", "col"), split_axis=1, concat_axis=1, tiled=True),
    )
    return result


def route_back(values):
    result = lax.all_to_all(values, ("row", "col"), split_axis=1, concat_axis=1, tiled=True)
    return result


def body(voltages, antenna_gains, receiving_tile_index, cell_index, beam_weights):
    channel_count, sample_count, antenna_local = (
        voltages.shape[0],
        voltages.shape[1],
        voltages.shape[3],
    )
    row_count, col_count, device_count = mesh_sizes()
    tile_capacity = 3 * antenna_local // device_count
    slot_count = device_count * tile_capacity
    tile_rows, tile_cols = (GRID_SIDE // row_count, GRID_SIDE // col_count)
    slab_rows = GRID_SIDE // device_count
    frame_count = channel_count * sample_count
    loss_factor = float(GRID_SIDE) ** 3 * math.sqrt(antenna_local * device_count)
    volt_re, volt_im = (voltages[:, :, 0], voltages[:, :, 1])
    calib_re = antenna_gains[0] * volt_re - antenna_gains[1] * volt_im
    calib_im = antenna_gains[0] * volt_im + antenna_gains[1] * volt_re
    calibrated = jnp.stack((calib_re, calib_im), -1).transpose(0, 2, 1, 3)
    tile_ids = receiving_tile_index[:, :, 0]
    onehot = (
        tile_ids[:, :, None] == jnp.arange(device_count, dtype=jnp.int32)[None, None, :]
    ).astype(jnp.float32)
    prior_result = (jnp.arange(antenna_local)[:, None] > jnp.arange(antenna_local)[None, :]).astype(
        jnp.float32
    )
    before = jnp.einsum("ab,cbd->cad", prior_result, onehot, preferred_element_type=jnp.float32)
    bucket_rank = jnp.sum(before * onehot, axis=2).astype(jnp.int32)
    position = tile_ids * tile_capacity + bucket_rank
    channel_ids = jnp.broadcast_to(
        jnp.arange(channel_count, dtype=jnp.int32)[:, None], position.shape
    )
    send_values = (
        jnp.zeros((channel_count, slot_count, sample_count, 2), jnp.float32)
        .at[channel_ids, position]
        .set(calibrated)
    )
    send_cells = (
        jnp.zeros((channel_count, slot_count), jnp.int32).at[channel_ids, position].set(cell_index)
    )
    got_values, got_cells = route_out(
        send_values.reshape(channel_count, device_count, tile_capacity, sample_count, 2),
        send_cells.reshape(channel_count, device_count, tile_capacity),
    )
    got_values = got_values.reshape(channel_count, slot_count, sample_count * 2)
    got_cells = got_cells.reshape(channel_count, slot_count)
    cell_row = got_cells // tile_cols
    cell_col = got_cells % tile_cols
    rows_tables = []
    cols_tables = []
    planes = []
    for channel in range(channel_count):
        rows_hot = (
            cell_row[channel][:, None] == jnp.arange(tile_rows, dtype=jnp.int32)[None, :]
        ).astype(jnp.float32)
        cols_hot = (
            cell_col[channel][:, None] == jnp.arange(tile_cols, dtype=jnp.int32)[None, :]
        ).astype(jnp.float32)
        rows_tables.append(rows_hot)
        cols_tables.append(cols_hot)
        for member in range(sample_count * 2):
            scaled = rows_hot * got_values[channel, :, member][:, None]
            planes.append(jnp.einsum("sr,sx->rx", scaled, cols_hot, precision=highest))
    blocks = jnp.stack(planes).reshape(frame_count, 2, col_count, slab_rows * tile_cols)
    spectrum = spectrum_move(column_move(blocks, rows_forward), columns_forward)
    spectrum_parts = spectrum.reshape(channel_count, sample_count, 2, slab_rows, GRID_SIDE)
    power_map = jnp.sum(
        spectrum_parts[:, :, 0] * spectrum_parts[:, :, 0]
        + spectrum_parts[:, :, 1] * spectrum_parts[:, :, 1],
        axis=1,
    )
    weighted = beam_weights * power_map
    power_total, power_square = lax.psum(
        (jnp.sum(weighted, axis=(1, 2)), jnp.sum(weighted * weighted, axis=(1, 2))), ("row", "col")
    )
    total_cell = power_total[:, None, None]
    weight = (
        2.0
        * loss_factor
        * beam_weights
        * ((weighted - power_square[:, None, None] / total_cell) / (total_cell * total_cell))
    )
    cotangent = 2.0 * weight[:, None, None] * spectrum_parts
    adjoint = spectrum_move(
        columns_adjoint(cotangent.reshape(frame_count, 2, slab_rows, GRID_SIDE)), rows_adjoint
    )
    tile_grad = column_move(adjoint, keep_blocks).reshape(
        channel_count, sample_count * 2, tile_rows, tile_cols
    )
    per_channel = []
    for channel in range(channel_count):
        members = []
        for member in range(sample_count * 2):
            picked = jnp.einsum(
                "sr,rx->sx", rows_tables[channel], tile_grad[channel, member], precision=highest
            )
            members.append(jnp.sum(picked * cols_tables[channel], axis=1))
        per_channel.append(jnp.stack(members, -1))
    slot_grad = jnp.stack(per_channel)
    returned_grad = route_back(
        slot_grad.reshape(channel_count, device_count, tile_capacity, sample_count, 2)
    ).reshape(channel_count, slot_count, sample_count, 2)
    own_grad = returned_grad[channel_ids, position]
    volt_pairs = voltages.transpose(0, 3, 1, 2)
    grad_re = jnp.sum(
        own_grad[..., 0] * volt_pairs[..., 0] + own_grad[..., 1] * volt_pairs[..., 1], axis=(0, 2)
    )
    grad_im = jnp.sum(
        own_grad[..., 1] * volt_pairs[..., 0] - own_grad[..., 0] * volt_pairs[..., 1], axis=(0, 2)
    )
    return jnp.stack((grad_re, grad_im))


def solution(mesh):
    placed = (
        P(None, None, None, ("row", "col")),
        P(None, ("row", "col")),
        P(None, ("row", "col"), None),
        P(None, ("row", "col")),
        P(None, ("row", "col"), None),
    )
    return jax.shard_map(
        body, mesh=mesh, in_specs=placed, out_specs=P(None, ("row", "col")), check_vma=False
    )
```

profile of v0, /device:TPU:1, one launch (start us, length us, event | category | flops | bytes accessed | tf_op | source)
XLA Modules:
  0.0 643.8 jit_solution(8985832388629105087)
XLA Ops:
  1.7 42.2 %scatter_fusion = s32[4,384]{1,0:T(4,128)S(1)} fusion(s32[4,384]{1,0:T(4,128)S(1)} %broadcast_in_dim.6, s32[512]{0:T(512)S(1)} %bitcast.362, s32[512]{0:T(512)} %bitcast.389), kind=kCustom, calls=%fused_computation.1 | custom fusion | bytes 10240 | tf_op jit(solution)/shard_map/scatter | solution.py:203
  45.0 11.5 %all-to-all-start = ((s32[4,128,3]{2,0,1:T(4,128)}), s32[4,128,3]{2,0,1:T(4,128)S(1)}, u32[]{:S(2)}, u32[]{:S(2)}) async-start(s32[4,128,3]{2,0,1:T(4,128)} %copy.142), calls=%async_computation | async-start | bytes 524288 | tf_op jit(solution)/shard_map/all_to_all | solution.py:157
  56.8 24.1 %scatter_fusion.1 = f32[4,384,2]{2,1,0:T(8,128)S(1)} fusion(f32[4,384,2]{2,1,0:T(8,128)S(1)} %broadcast.746, s32[512]{0:T(512)S(1)} %bitcast.363, f32[512,2]{1,0:T(8,128)S(1)} %bitcast.384), kind=kCustom, calls=%fused_computation.2 | custom fusion | bytes 16384 | tf_op jit(solution)/shard_map/scatter | solution.py:200
  84.0 10.2 %all-to-all-start.1 = ((f32[4,128,3,1,2]{0,4,3,2,1:T(2,128)}), f32[4,128,3,1,2]{0,4,3,2,1:T(2,128)S(1)}, u32[]{:S(2)}, u32[]{:S(2)}) async-start(f32[4,128,3,1,2]{0,4,3,2,1:T(2,128)} %bitcast.23), calls=%async_computation.1 | async-start | bytes 786432 | tf_op jit(solution)/shard_map/all_to_all | solution.py:156
  94.5 11.4 %all-to-all-done.1 = f32[4,128,3,1,2]{0,4,3,2,1:T(2,128)S(1)} async-done(((f32[4,128,3,1,2]{0,4,3,2,1:T(2,128)}), f32[4,128,3,1,2]{0,4,3,2,1:T(2,128)S(1)}, u32[]{:S(2)}, u32[]{:S(2)}) %all-to-all-start.1) | async-done | bytes 12320 | tf_op jit(solution)/shard_map/all_to_all | solution.py:156
  105.9 11.0 %slice_reduce_fusion = (f32[384]{0:T(512)S(1)}, f32[384]{0:T(512)S(1)}, f32[384]{0:T(512)S(1)}, f32[384]{0:T(512)S(1)}, f32[384]{0:T(512)S(1)}, /*index=5*/f32[384]{0:T(512)S(1)}, f32[384]{0:T(512)S(1)}, f32[384]{0:T(512)S(1)}) fusion(f32[4,384,2]{0,2,1:T(2,128)S(1)} %bitcast.374), kind=kLoop, calls=%fused_computation.167 | loop fusion | bytes 24576 | tf_op jit(solution)/shard_map/slice | solution.py:226
  130.6 4.9 reshape.741
  135.5 7.4 %copy.149 = f32[4,2,8,16384]{3,1,0,2:T(2,128)} copy(f32[4,2,8,16384]{3,2,1,0:T(8,128)} %reshape.741) | data formatting | bytes 8388608 | tf_op jit(solution)/shard_map/reshape | solution.py:228
  142.9 5.4 all-to-all-start.2
  148.4 48.7 %all-to-all-done.2 = f32[4,2,8,16384]{3,1,0,2:T(2,128)} async-done(((f32[4,2,8,16384]{3,1,0,2:T(2,128)}), f32[4,2,8,16384]{3,1,0,2:T(2,128)}, u32[]{:S(2)}, u32[]{:S(2)}) %all-to-all-start.2) | async-done | bytes 4194336 | tf_op jit(solution)/shard_map/all_to_all | solution.py:144
  197.1 7.3 %reshape.803 = f32[4,2,8,32,4,128]{5,4,3,1,0,2:T(4,128)} reshape(f32[4,2,8,16384]{3,1,0,2:T(2,128)} %all-to-all-done.2) | data formatting | bytes 8388608 | tf_op jit(solution)/shard_map/reshape | solution.py:55
  232.4 5.6 fusion.78
  241.3 4.9 pad_maximum_fusion
  246.2 5.5 all-to-all-start.3
  251.8 52.6 %all-to-all-done.3 = f32[4,2,128,1024]{3,0,1,2:T(4,128)} async-done(((f32[4,2,128,1024]{3,0,1,2:T(4,128)}), f32[4,2,128,1024]{3,0,1,2:T(4,128)}, u32[]{:S(2)}, u32[]{:S(2)}) %all-to-all-start.3) | async-done | bytes 4194336 | tf_op jit(solution)/shard_map/all_to_all | solution.py:149
  304.4 5.4 copy.155
  309.9 3.9 fusion.26
  330.0 4.7 fusion.12
  337.4 3.8 multiply_reduce_fusion
  341.3 62.9 %all-reduce = (f32[4]{0:T(128)S(1)}, f32[4]{0:T(128)S(1)}) all-reduce(f32[4]{0:T(128)S(1)} %get-tuple-element.6, f32[4]{0:T(128)S(1)} %get-tuple-element.5), channel_id=1, replica_groups=mesh['row'=16,'col'=8] {'row','col'}, use_global_device_ids=true, to_apply=%region_6.7 | all-reduce | flops 8 | bytes 64 | tf_op jit(solution)/shard_map/psum | solution.py:237
  421.0 4.4 fusion.37
  425.4 4.5 fusion.65
  433.1 5.2 fusion.68
  444.3 58.0 %all_to_all.35 = f32[4,2,128,1024]{3,0,1,2:T(4,128)} all-to-all(f32[4,2,128,1024]{3,0,1,2:T(4,128)S(1)} %pad_maximum_fusion.1), channel_id=1, replica_groups=mesh['row'=16,'col'=8] {'row','col'}, dimensions={2} | all-to-all | bytes 8388608 | tf_op jit(solution)/shard_map/all_to_all | solution.py:149
  502.3 5.5 copy.170
  507.8 3.9 fusion.34
  520.0 3.9 fusion
  531.9 4.3 add_bitcast_fusion
  544.9 52.3 %all_to_all.36 = f32[4,2,8,16384]{3,0,1,2:T(4,128)S(1)} all-to-all(f32[4,2,8,16384]{3,0,1,2:T(4,128)S(1)} %copy.173), channel_id=1, replica_groups=mesh['row'=16,'col'=8] {'col'}, dimensions={2} | all-to-all | bytes 8388608 | tf_op jit(solution)/shard_map/all_to_all | solution.py:144
  597.1 4.4 copy.174
  601.5 5.0 reshape.751
  619.5 16.6 %all_to_all.37 = f32[4,128,3,1,2]{0,4,3,2,1:T(2,128)S(1)} all-to-all(f32[4,128,3,1,2]{0,4,3,2,1:T(2,128)S(1)} %copy.175), channel_id=1, replica_groups=mesh['row'=16,'col'=8] {'row','col'}, dimensions={1} | all-to-all | bytes 24576 | tf_op jit(solution)/shard_map/all_to_all | solution.py:163
  (114 shorter events, 141.6 us)
Async XLA Ops:
  1.7 54.8 %copy-start.8 = (f32[4,1,2,128]{3,2,1,0:T(2,128)S(1)}, f32[4,1,2,128]{3,2,1,0:T(2,128)}, u32[]{:S(2)}) copy-start(f32[4,1,2,128]{3,2,1,0:T(2,128)} %param.5) | copy-start | bytes 12292
  1.7 54.8 %copy-start.9 = (f32[2,128]{1,0:T(2,128)S(1)}, f32[2,128]{1,0:T(2,128)}, u32[]{:S(2)}) copy-start(f32[2,128]{1,0:T(2,128)} %param.6) | copy-start | bytes 3076
  45.0 39.0 %all-to-all-start = ((s32[4,128,3]{2,0,1:T(4,128)}), s32[4,128,3]{2,0,1:T(4,128)S(1)}, u32[]{:S(2)}, u32[]{:S(2)}) async-start(s32[4,128,3]{2,0,1:T(4,128)} %copy.142), calls=%async_computation | async-start | bytes 524288 | tf_op jit(solution)/shard_map/all_to_all | solution.py:157
  84.0 22.0 %all-to-all-start.1 = ((f32[4,128,3,1,2]{0,4,3,2,1:T(2,128)}), f32[4,128,3,1,2]{0,4,3,2,1:T(2,128)S(1)}, u32[]{:S(2)}, u32[]{:S(2)}) async-start(f32[4,128,3,1,2]{0,4,3,2,1:T(2,128)} %bitcast.23), calls=%async_computation.1 | async-start | bytes 786432 | tf_op jit(solution)/shard_map/all_to_all | solution.py:156
  142.9 54.2 %all-to-all-start.2 = ((f32[4,2,8,16384]{3,1,0,2:T(2,128)}), f32[4,2,8,16384]{3,1,0,2:T(2,128)}, u32[]{:S(2)}, u32[]{:S(2)}) async-start(f32[4,2,8,16384]{3,1,0,2:T(2,128)} %copy.149), calls=%async_computation.2 | async-start | bytes 8388608 | tf_op jit(solution)/shard_map/all_to_all | solution.py:144
  220.2 5.6 copy-start.1
  238.0 3.3 copy-start.5
  246.2 58.2 %all-to-all-start.3 = ((f32[4,2,128,1024]{3,0,1,2:T(4,128)}), f32[4,2,128,1024]{3,0,1,2:T(4,128)}, u32[]{:S(2)}, u32[]{:S(2)}) async-start(f32[4,2,128,1024]{3,0,1,2:T(4,128)} %pad_maximum_fusion), calls=%async_computation.3 | async-start | bytes 8388608 | tf_op jit(solution)/shard_map/all_to_all | solution.py:149
  309.9 3.9 copy-start.2
  406.8 1.6 copy-start.4
  438.3 3.3 copy-start.6
  507.8 3.9 copy-start.3
  517.9 6.0 copy-start
  606.4 7.0 %copy-start.7 = (f32[4,2,256,512]{3,2,1,0:T(8,128)S(1)}, f32[4,2,256,512]{3,2,1,0:T(8,128)}, u32[]{:S(2)}) copy-start(f32[4,2,256,512]{3,2,1,0:T(8,128)} %reshape.751) | copy-start | bytes 12582916
where the time goes:
time: 650 us; the launch traced here: 644 us
  blocking collectives  190 us (29%)
  local copies, waits for them, and re-layouts  164 us (25%)
  matrix products  125 us (19%)
  waiting for transfers between devices  113 us (17%)
  starting transfers between devices  32.6 us (5%)
  other arithmetic  18.9 us (3%)
    psum x1, blocking collectives, body(): lax.psum((jnp.sum(weighted, axis=(1, 2)), jnp.sum(weighted * weighted, ax...  62.9 us
    all_to_all x1, blocking collectives, spectrum_move(): lax.all_to_all(blocks, ('row', 'col'), split_axis=2, concat_axis=2, tiled...  58 us
    all_to_all x1, waiting for transfers between devices, spectrum_move(): lax.all_to_all(blocks, ('row', 'col'), split_axis=2, concat_axis=2, tiled...  52.6 us
    all_to_all x1, blocking collectives, column_move(): lax.all_to_all(blocks, 'col', split_axis=2, concat_axis=2, tiled=True)  52.3 us
    all_to_all x1, waiting for transfers between devices, column_move(): lax.all_to_all(blocks, 'col', split_axis=2, concat_axis=2, tiled=True)  48.7 us
    scatter x1, local copies, waits for them, and re-layouts, body(): jnp.zeros((channel_count, slot_count), jnp.int32).at[channel_ids, position]  42.2 us
    dot_general x8, matrix products, complex_einsum(): jnp.einsum(pattern, factor[0], phases[1], precision=highest)  29.1 us
    dot_general x8, matrix products, complex_einsum(): jnp.einsum(pattern, factor[0], phases[0], precision=highest)  26.1 us
  transfers between devices with their start and end apart: 4, of which 3 were waited for; matrix products, arithmetic and copies ran while one was open for 4% of the time, Pallas kernels for 0%

commit v1 on v0

v1 whole, which is shorter than its diff:
```python
import math

import jax
import jax.numpy as jnp
import numpy as np
from jax import lax
from jax.experimental import pallas as pl
from jax.experimental.pallas import tpu as pltpu
from jax.sharding import PartitionSpec as P

GRID = 4096
AXES = ("row", "col")
CHANNELS = 4
LANES = 128
SOURCES = 128
BUCKETS = 16
CAP = 24
SLOTS = BUCKETS * CAP
WIDTH = 32
ROWS = 256

f32 = jnp.float32
bf16 = jnp.bfloat16
i32 = jnp.int32
NT = (((1,), (1,)), ((), ()))
NN = (((1,), (0,)), ((), ()))


def split_table(values):
    high = values.astype(np.float32).astype(jnp.bfloat16)
    low = (values - high.astype(np.float64)).astype(np.float32).astype(jnp.bfloat16)
    return high, low


def dft_tables():
    n = np.arange(ROWS)
    angle = 2.0 * np.pi * (np.outer(n, n) % ROWS) / ROWS
    cos, sin = np.cos(angle), np.sin(angle)
    matrix = np.block([[cos, -sin], [sin, cos]])
    high, low = split_table(matrix)
    turn = 2.0 * np.pi * np.outer(np.arange(BUCKETS), n) / GRID
    twiddle = np.stack([np.cos(turn), -np.sin(turn)]).astype(np.float32)
    return high, low, twiddle


def cmul(a, b):
    return (a[0] * b[0] - a[1] * b[1], a[0] * b[1] + a[1] * b[0])


def cadd(a, b):
    return (a[0] + b[0], a[1] + b[1])


def csub(a, b):
    return (a[0] - b[0], a[1] - b[1])


def cturn(a, sign):
    return (-a[1], a[0]) if sign > 0 else (a[1], -a[0])


def radix4(x, sign):
    s0, d0 = cadd(x[0], x[2]), csub(x[0], x[2])
    s1, d1 = cadd(x[1], x[3]), cturn(csub(x[1], x[3]), sign)
    return [cadd(s0, s1), cadd(d0, d1), csub(s0, s1), csub(d0, d1)]


def radix16(x, sign):
    inner = [radix4([x[4 * a + b] for a in range(4)], sign) for b in range(4)]
    out = [None] * 16
    for low in range(4):
        terms = []
        for b in range(4):
            value = inner[b][low]
            turns = (b * low) % 16
            if turns == 4:
                value = cturn(value, sign)
            elif turns:
                angle = sign * 2.0 * math.pi * turns / 16
                value = cmul(value, (math.cos(angle), math.sin(angle)))
            terms.append(value)
        result = radix4(terms, sign)
        for m in range(4):
            out[low + 4 * m] = result[m]
    return out


def unit_phase(steps):
    quarter = (steps + 512) >> 10
    x = (steps - (quarter << 10)).astype(f32) * (2.0 * math.pi / GRID)
    x2 = x * x
    sin = x * (1.0 + x2 * (-1.0 / 6 + x2 * (1.0 / 120 + x2 * (-1.0 / 5040 + x2 * (1.0 / 362880)))))
    cos = 1.0 + x2 * (
        -0.5 + x2 * (1.0 / 24 + x2 * (-1.0 / 720 + x2 * (1.0 / 40320 - x2 * (1.0 / 3628800))))
    )
    swap = (quarter & 1) == 1
    real = jnp.where(swap, sin, cos)
    imag = jnp.where(swap, cos, sin)
    real = jnp.where(((quarter + 1) & 2) == 2, -real, real)
    imag = jnp.where((quarter & 2) == 2, -imag, imag)
    return real, -imag


def lane_pick(values, index):
    return jnp.take_along_axis(values, index, axis=1)


def pack_kernel(volt_ref, gain_ref, tile_ref, cell_ref, message_ref, place_ref):
    lane = lax.broadcasted_iota(i32, (1, LANES), 1)
    down = lax.broadcasted_iota(i32, (LANES, LANES), 0).astype(f32)
    rows = [[], [], [], []]
    for c in range(CHANNELS):
        tile = tile_ref[c : c + 1, :]
        cell = cell_ref[c : c + 1, :]
        key = ((tile >> 3) * LANES + lane).astype(f32)
        key_across = jnp.broadcast_to(key, (LANES, LANES))
        key_down = key_across.T
        place = jnp.sum(jnp.where(key_down < key_across, 1.0, 0.0), axis=0, keepdims=True)
        place_ref[c : c + 1, :] = place.astype(i32)
        order = jnp.where(down == place, 1.0, 0.0)
        vr, vi = volt_ref[2 * c : 2 * c + 1, :], volt_ref[2 * c + 1 : 2 * c + 2, :]
        gr, gi = gain_ref[0:1, :], gain_ref[1:2, :]
        grid_row = ((tile >> 3) * ROWS + (cell >> 9)).astype(f32)
        grid_col = ((tile & 7) * 512 + (cell & 511)).astype(f32)
        features = jnp.concatenate(
            [gr * vr - gi * vi, gr * vi + gi * vr, grid_row, grid_col, jnp.zeros((4, LANES), f32)], 0
        )
        ordered = lax.dot_general(
            features, order, NT, precision=lax.Precision.HIGHEST, preferred_element_type=f32
        )
        for f in range(4):
            rows[f].append(ordered[f : f + 1, :])
    message = jnp.concatenate([row for group in rows for row in group], 0)

    def put(d, carry):
        message_ref[d] = message
        return carry

    lax.fori_loop(0, SOURCES, put, 0, unroll=8)


def slot_kernel(got_ref, vr_ref, vi_ref, row_ref, col_ref, back_ref, most_ref, buf, sems):
    outs = (vr_ref, vi_ref, row_ref, col_ref)

    def copies():
        return [
            pltpu.make_async_copy(got_ref.at[:, k, :], buf.at[k], sems.at[k]) for k in range(16)
        ]

    for copy in copies():
        copy.start()
    for copy in copies():
        copy.wait()
    lane = lax.broadcasted_iota(i32, (LANES, LANES), 1)
    most_ref[...] = jnp.zeros((8, LANES), i32)
    for c in range(CHANNELS):
        bucket = buf[8 + c].astype(i32) >> 8
        start = jnp.zeros((LANES, LANES), i32)
        for step in (64, 32, 16, 8, 4, 2, 1, 1):
            probe = start + step
            seen = lane_pick(bucket, probe - 1)
            start = jnp.where(seen < lane, probe, start)
        count = pltpu.roll(start, LANES - 1, axis=1) - start
        most_ref[c : c + 1, :] = jnp.max(count, axis=0, keepdims=True)
        back_ref[c] = bucket * CAP + lane - lane_pick(start, bucket)
        for t in range(3):
            slot = lane + t * LANES
            owner = (slot * 2731) >> 16
            rank = slot - owner * CAP
            source = jnp.minimum(lane_pick(start, owner) + rank, LANES - 1)
            valid = rank < lane_pick(count, owner)
            for f in range(4):
                picked = lane_pick(buf[4 * f + c], source)
                if f == 2:
                    picked = picked - owner.astype(f32) * ROWS
                picked = jnp.where(valid, picked, 0.0)
                outs[f][pl.ds(c * SLOTS + t * LANES, LANES), :] = picked.T


def fill_iota(iota_ref):
    iota_ref[...] = lax.broadcasted_iota(i32, (ROWS, LANES), 0).astype(f32).astype(bf16)


def one_hot(row_ref, iota_ref, at):
    want = jnp.broadcast_to(row_ref[pl.ds(at, 1), :], (16, LANES)).astype(bf16)
    one, zero = jnp.ones((16, LANES), bf16), jnp.zeros((16, LANES), bf16)
    return jnp.concatenate(
        [jnp.where(iota_ref[16 * i : 16 * i + 16, :] == want, one, zero) for i in range(ROWS // 16)], 0
    )


def two_terms(x):
    high = x.astype(bf16)
    return high, (x - high.astype(f32)).astype(bf16)


def phase_rows(tile, base, first, col_ref, br, bi, zr, zi, value=None):
    at = pl.multiple_of(base + 8 * tile, 8)
    col = col_ref[pl.ds(at, 8), :].astype(i32)
    b0 = unit_phase((col * first) & (GRID - 1))
    if value is not None:
        b0 = cmul((value[0][pl.ds(at, 8), :], value[1][pl.ds(at, 8), :]), b0)
    w1 = unit_phase(col)
    w2 = cmul(w1, w1)
    w4 = cmul(w2, w2)
    w8 = cmul(w4, w4)
    b = [b0, cmul(b0, w1)]
    b += [cmul(x, w2) for x in b]
    b += [cmul(x, w4) for x in b]
    for s in range(8):
        to = pl.multiple_of(64 * tile + 8 * s, 8)
        br[pl.ds(to, 8), :] = b[s][0]
        bi[pl.ds(to, 8), :] = b[s][1]
    to = pl.multiple_of(8 * tile, 8)
    zr[pl.ds(to, 8), :] = w8[0]
    zi[pl.ds(to, 8), :] = w8[1]


def load_phases(rank, br, bi, zr, zi):
    tile, inner = rank >> 3, rank & 7
    b = (br[pl.ds(64 * tile + inner, 8, stride=8), :], bi[pl.ds(64 * tile + inner, 8, stride=8), :])
    z = (
        jnp.broadcast_to(zr[pl.ds(rank, 1), :], (8, LANES)),
        jnp.broadcast_to(zi[pl.ds(rank, 1), :], (8, LANES)),
    )
    return b, z


def forward_kernel(
    most_ref, first_ref, vr_ref, vi_ref, row_ref, col_ref, beam_ref, high_ref, low_ref, tw_ref,
    spec_ref, sums_ref, br, bi, zr, zi, acc, grid, dh, dl, iota_ref,
):
    fill_iota(iota_ref)
    first = first_ref[0]

    def bucket_step(cp, carry):
        base = cp * CAP
        most = jnp.minimum(most_ref[cp >> 4, cp & 15], CAP)

        def tiles(t, carry):
            phase_rows(t, base, first, col_ref, br, bi, zr, zi, (vr_ref, vi_ref))
            return carry

        lax.fori_loop(0, (most + 7) >> 3, tiles, 0)
        acc[...] = jnp.zeros((128, ROWS), f32)

        def chunk(k, carry):
            left, right = [], []
            for h in range(2):
                rank = 2 * k + h
                x, z = load_phases(rank, br, bi, zr, zi)
                parts = [x]
                for _ in range(3):
                    x = cmul(x, z)
                    parts.append(x)
                value = jnp.concatenate([v[0] for v in parts] + [v[1] for v in parts], 0)
                left.append(jnp.concatenate(two_terms(value), 0))
                right.append(one_hot(row_ref, iota_ref, base + rank))
            acc[...] += lax.dot_general(
                jnp.concatenate(left, 1), jnp.concatenate(right, 1), NT, preferred_element_type=f32
            )
            return carry

        lax.fori_loop(0, (most + 1) >> 1, chunk, 0)
        grid[pl.ds(pl.multiple_of(cp * 64, 64), 64), :] = acc[0:64, :] + acc[64:128, :]
        return carry

    lax.fori_loop(0, CHANNELS * BUCKETS, bucket_step, 0)

    lane = lax.broadcasted_iota(i32, (1, LANES), 1)
    sums = jnp.zeros((1, LANES), f32)
    for c in range(CHANNELS):
        for half in range(2):
            across = slice(half * LANES, half * LANES + LANES)

            def columns(t, carry):
                x = []
                for b in range(BUCKETS):
                    at = (c * BUCKETS + b) * 64
                    x.append(
                        (
                            grid[pl.ds(pl.multiple_of(at + 8 * t, 8), 8), across],
                            grid[pl.ds(pl.multiple_of(at + 32 + 8 * t, 8), 8), across],
                        )
                    )
                y = radix16(x, -1)
                for k in range(BUCKETS):
                    turn = (
                        jnp.broadcast_to(tw_ref[0, k : k + 1, across], (8, LANES)),
                        jnp.broadcast_to(tw_ref[1, k : k + 1, across], (8, LANES)),
                    )
                    value = cmul(y[k], turn) if k else y[k]
                    at = (c * BUCKETS + k) * 64
                    grid[pl.ds(pl.multiple_of(at + 8 * t, 8), 8), across] = value[0]
                    grid[pl.ds(pl.multiple_of(at + 32 + 8 * t, 8), 8), across] = value[1]
                return carry

            lax.fori_loop(0, 4, columns, 0)
        for k in range(BUCKETS):
            at = (c * BUCKETS + k) * 64
            for part in range(2):
                high, low = two_terms(grid[at + 32 * part : at + 32 * part + 32, :])
                dh[32 * k : 32 * k + 32, ROWS * part : ROWS * part + ROWS] = high
                dl[32 * k : 32 * k + 32, ROWS * part : ROWS * part + ROWS] = low
        spec = (
            lax.dot_general(dh[...], high_ref[...], NN, preferred_element_type=f32)
            + lax.dot_general(dl[...], high_ref[...], NN, preferred_element_type=f32)
            + lax.dot_general(dh[...], low_ref[...], NN, preferred_element_type=f32)
        )
        spec_ref[c] = spec
        re, im = spec[:, 0:ROWS], spec[:, ROWS : 2 * ROWS]
        weighted = beam_ref[c] * (re * re + im * im)
        total = jnp.sum(jnp.sum(weighted, axis=0, keepdims=True), axis=1, keepdims=True)
        square = jnp.sum(jnp.sum(weighted * weighted, axis=0, keepdims=True), axis=1, keepdims=True)
        sums = jnp.where(lane == c, total, sums)
        sums = jnp.where(lane == CHANNELS + c, square, sums)

    def put(d, carry):
        sums_ref[d] = sums
        return carry

    lax.fori_loop(0, SOURCES, put, 0, unroll=8)


def adjoint_kernel(
    most_ref, first_ref, sums_ref, row_ref, col_ref, back_ref, beam_ref, high_ref, low_ref, tw_ref,
    spec_ref, out_ref, br, bi, zr, zi, tr, ti, gr, gi, grid, dh, dl, left, iota_ref,
):
    fill_iota(iota_ref)
    first = first_ref[0]
    sums = jnp.sum(sums_ref[...], axis=0)
    loss_factor = float(GRID) ** 3 * math.sqrt(SOURCES * LANES)
    for c in range(CHANNELS):
        total, square = sums[:, c : c + 1], sums[:, CHANNELS + c : CHANNELS + c + 1]
        mean = square / total
        scale = (4.0 * loss_factor) / (total * total)
        for k in range(BUCKETS):
            rows = slice(32 * k, 32 * k + 32)
            re, im = spec_ref[c, rows, 0:ROWS], spec_ref[c, rows, ROWS : 2 * ROWS]
            beam = beam_ref[c, rows, :]
            weight = beam * ((beam * (re * re + im * im) - mean) * scale)
            for part, value in enumerate((weight * re, weight * im)):
                high, low = two_terms(value)
                dh[rows, ROWS * part : ROWS * part + ROWS] = high
                dl[rows, ROWS * part : ROWS * part + ROWS] = low
        spread = (
            lax.dot_general(dh[...], high_ref[...], NT, preferred_element_type=f32)
            + lax.dot_general(dl[...], high_ref[...], NT, preferred_element_type=f32)
            + lax.dot_general(dh[...], low_ref[...], NT, preferred_element_type=f32)
        )
        for k in range(BUCKETS):
            at = (c * BUCKETS + k) * 64
            grid[at : at + 32, :] = spread[32 * k : 32 * k + 32, 0:ROWS]
            grid[at + 32 : at + 64, :] = spread[32 * k : 32 * k + 32, ROWS : 2 * ROWS]
        for half in range(2):
            across = slice(half * LANES, half * LANES + LANES)

            def columns(t, carry):
                x = []
                for k in range(BUCKETS):
                    turn = (
                        jnp.broadcast_to(tw_ref[0, k : k + 1, across], (8, LANES)),
                        -jnp.broadcast_to(tw_ref[1, k : k + 1, across], (8, LANES)),
                    )
                    at = (c * BUCKETS + k) * 64
                    value = (
                        grid[pl.ds(pl.multiple_of(at + 8 * t, 8), 8), across],
                        grid[pl.ds(pl.multiple_of(at + 32 + 8 * t, 8), 8), across],
                    )
                    x.append(cmul(value, turn) if k else value)
                y = radix16(x, 1)
                for b in range(BUCKETS):
                    at = (c * BUCKETS + b) * 64
                    grid[pl.ds(pl.multiple_of(at + 8 * t, 8), 8), across] = y[b][0]
                    grid[pl.ds(pl.multiple_of(at + 32 + 8 * t, 8), 8), across] = y[b][1]
                return carry

            lax.fori_loop(0, 4, columns, 0)

    def bucket_step(cp, carry):
        base = cp * CAP
        most = jnp.minimum(most_ref[cp >> 4, cp & 15], CAP)
        tiles_used = (most + 7) >> 3

        def tiles(t, carry):
            phase_rows(t, base, first, col_ref, br, bi, zr, zi)
            return carry

        lax.fori_loop(0, tiles_used, tiles, 0)
        high, low = two_terms(grid[pl.ds(pl.multiple_of(cp * 64, 64), 64), :])
        left[0:64, :] = high
        left[64:128, :] = low

        def chunk(k, carry):
            right = jnp.concatenate([one_hot(row_ref, iota_ref, base + 2 * k + h) for h in range(2)], 1)
            both = lax.dot_general(left[...], right, NN, preferred_element_type=f32)
            both = both[0:64, :] + both[64:128, :]
            for h in range(2):
                rank = 2 * k + h
                b, z = load_phases(rank, br, bi, zr, zi)
                g = both[:, h * LANES : h * LANES + LANES]
                a = (g[24:32, :], g[56:64, :])
                for m in (2, 1, 0):
                    a = (
                        g[8 * m : 8 * m + 8, :] + (a[0] * z[0] + a[1] * z[1]),
                        g[32 + 8 * m : 40 + 8 * m, :] + (a[1] * z[0] - a[0] * z[1]),
                    )
                to = pl.multiple_of(8 * rank, 8)
                tr[pl.ds(to, 8), :] = a[0] * b[0] + a[1] * b[1]
                ti[pl.ds(to, 8), :] = a[1] * b[0] - a[0] * b[1]
            return carry

        lax.fori_loop(0, (most + 1) >> 1, chunk, 0)

        def gather(t, carry):
            to = pl.multiple_of(base + 8 * t, 8)
            for source, target in ((tr, gr), (ti, gi)):
                value = source[pl.ds(64 * t, 8, stride=8), :]
                for s in range(1, 8):
                    value = value + source[pl.ds(64 * t + s, 8, stride=8), :]
                target[pl.ds(to, 8), :] = value
            return carry

        lax.fori_loop(0, tiles_used, gather, 0)
        return carry

    lax.fori_loop(0, CHANNELS * BUCKETS, bucket_step, 0)

    for c in range(CHANNELS):
        index = back_ref[c]
        inner, block = index & (LANES - 1), index >> 7
        for part, source in enumerate((gr, gi)):
            value = None
            for t in range(3):
                at = c * SLOTS + t * LANES
                picked = lane_pick(source[at : at + LANES, :].T, inner)
                value = picked if value is None else jnp.where(block == t, picked, value)
            out_ref[:, part * CHANNELS + c, :] = value


def finish_kernel(got_ref, place_ref, volt_ref, out_ref):
    grad = jnp.sum(got_ref[...], axis=0)
    place = place_ref[...]
    grad = lane_pick(grad, jnp.concatenate([place, place], 0))
    real = jnp.zeros((1, LANES), f32)
    imag = jnp.zeros((1, LANES), f32)
    for c in range(CHANNELS):
        g_re, g_im = grad[c : c + 1, :], grad[CHANNELS + c : CHANNELS + c + 1, :]
        v_re, v_im = volt_ref[2 * c : 2 * c + 1, :], volt_ref[2 * c + 1 : 2 * c + 2, :]
        real = real + g_re * v_re + g_im * v_im
        imag = imag + g_im * v_re - g_re * v_im
    out_ref[...] = jnp.concatenate([real, imag], 0)


def exchange(message):
    return lax.all_to_all(message, AXES, split_axis=0, concat_axis=0, tiled=True)


def shape(dims, dtype=f32):
    return jax.ShapeDtypeStruct(dims, dtype)


VMEM = pl.BlockSpec(memory_space=pltpu.VMEM)
SMEM = pl.BlockSpec(memory_space=pltpu.SMEM)
LARGE = pltpu.CompilerParams(vmem_limit_bytes=56 * 1024 * 1024)


def body(voltages, antenna_gains, receiving_tile_index, cell_index, beam_weights):
    high, low, twiddle = (jnp.asarray(t) for t in dft_tables())
    device = lax.axis_index("row") * lax.axis_size("col") + lax.axis_index("col")
    first = (device * WIDTH).astype(i32).reshape(1)
    volts = voltages.reshape(2 * CHANNELS, LANES)
    tiles = receiving_tile_index.reshape(CHANNELS, LANES)
    message, place = pl.pallas_call(
        pack_kernel,
        out_shape=(shape((SOURCES, 16, LANES)), shape((CHANNELS, LANES), i32)),
        in_specs=[VMEM] * 4,
        out_specs=(VMEM, VMEM),
    )(volts, antenna_gains, tiles, cell_index)
    got = exchange(message)
    beam = beam_weights.reshape(CHANNELS, WIDTH, ROWS, BUCKETS).transpose(0, 3, 1, 2)
    beam = beam.reshape(CHANNELS, BUCKETS * WIDTH, ROWS)
    slot = shape((CHANNELS * SLOTS, LANES))
    val_re, val_im, rows, cols, back, most = pl.pallas_call(
        slot_kernel,
        out_shape=(slot, slot, slot, slot, shape((CHANNELS, SOURCES, LANES), i32), shape((8, LANES), i32)),
        in_specs=[pl.BlockSpec(memory_space=pl.ANY)],
        out_specs=(VMEM,) * 6,
        scratch_shapes=[pltpu.VMEM((16, SOURCES, LANES), f32), pltpu.SemaphoreType.DMA((16,))],
        compiler_params=LARGE,
    )(got)
    phases = [
        pltpu.VMEM((CAP * 8, LANES), f32),
        pltpu.VMEM((CAP * 8, LANES), f32),
        pltpu.VMEM((CAP, LANES), f32),
        pltpu.VMEM((CAP, LANES), f32),
    ]
    planes = [
        pltpu.VMEM((CHANNELS * BUCKETS * 64, ROWS), f32),
        pltpu.VMEM((512, 512), bf16),
        pltpu.VMEM((512, 512), bf16),
    ]
    spectrum, sums = pl.pallas_call(
        forward_kernel,
        out_shape=(shape((CHANNELS, 512, 512)), shape((SOURCES, 1, LANES))),
        in_specs=[SMEM, SMEM] + [VMEM] * 8,
        out_specs=(VMEM, VMEM),
        scratch_shapes=phases
        + [pltpu.VMEM((128, ROWS), f32)]
        + planes
        + [pltpu.VMEM((ROWS, LANES), bf16)],
        compiler_params=LARGE,
    )(most, first, val_re, val_im, rows, cols, beam, high, low, twiddle)
    sums = exchange(sums)
    partial = pl.pallas_call(
        adjoint_kernel,
        out_shape=shape((SOURCES, 8, LANES)),
        in_specs=[SMEM, SMEM] + [VMEM] * 9,
        out_specs=VMEM,
        scratch_shapes=phases
        + [pltpu.VMEM((CAP * 8, LANES), f32)] * 2
        + [pltpu.VMEM((CHANNELS * SLOTS, LANES), f32)] * 2
        + planes
        + [pltpu.VMEM((128, ROWS), bf16), pltpu.VMEM((ROWS, LANES), bf16)],
        compiler_params=LARGE,
    )(most, first, sums, rows, cols, back, beam, high, low, twiddle, spectrum)
    home = exchange(partial)
    return pl.pallas_call(
        finish_kernel,
        out_shape=shape((2, LANES)),
        in_specs=[VMEM] * 3,
        out_specs=VMEM,
    )(home, place, volts)


def solution(mesh):
    placed = (
        P(None, None, None, AXES),
        P(None, AXES),
        P(None, AXES, None),
        P(None, AXES),
        P(None, AXES, None),
    )
    return jax.shard_map(body, mesh=mesh, in_specs=placed, out_specs=P(None, AXES), check_vma=False)
```

time: 650 us -> 243 us (0.37)
  Pallas kernels: 0 us -> 176 us
  blocking collectives: 190 us -> 34.2 us
  local copies, waits for them, and re-layouts: 164 us -> 14.5 us
  matrix products: 125 us -> 0 us
  waiting for transfers between devices: 113 us -> 5.74 us
  starting transfers between devices: 32.6 us -> 11.5 us
  other arithmetic: 18.9 us -> 0 us
    pallas_call x0 -> x5, Pallas kernels: none -> 176 us  [the longest x1 82.4 us: body(): pl.pallas_call(forward_kernel, out_shape=(shape((CHANNELS, 512, 512)), sh...]
    dot_general x49 -> x0, matrix products: 125 us -> none  [the longest x8 29.1 us: complex_einsum(): jnp.einsum(pattern, factor[0], phases[1], precision=highest)]
    all_to_all x4 -> x1, waiting for transfers between devices: 113 us -> 5.74 us  [exchange(): lax.all_to_all(message, AXES, split_axis=0, concat_axis=0, tiled=True)]
    all_to_all x3 -> x2, blocking collectives: 127 us -> 34.2 us  [exchange(): lax.all_to_all(message, AXES, split_axis=0, concat_axis=0, tiled=True)]
    scatter x2 -> x0, local copies, waits for them, and re-layouts: 66.3 us -> none  [the longest x1 42.2 us: body(): jnp.zeros((channel_count, slot_count), jnp.int32).at[channel_ids, position]]
    psum x1 -> x0, blocking collectives: 62.9 us -> none  [body(): lax.psum((jnp.sum(weighted, axis=(1, 2)), jnp.sum(weighted * weighted, ax...]
    reshape x9 -> x0, local copies, waits for them, and re-layouts: 31.9 us -> none  [the longest x2 12.3 us: body(): jnp.stack(planes).reshape(frame_count, 2, col_count, slab_rows * tile_cols)]
    another operation x16 -> x0, local copies, waits for them, and re-layouts: 24 us -> none  [the longest x3 7.94 us: rows_adjoint(): jnp.stack(result, 1)]
  transfers between devices with their start and end apart: 4 -> 1, of which waited for: 3 -> 1; matrix products, arithmetic and copies ran while one was open for 4% -> 6% of each run, Pallas kernels for 0% -> 0%
where the time goes in v1:
time: 243 us; the launch traced here: 242 us
  Pallas kernels  176 us (72%)
  blocking collectives  34.2 us (14%)
  local copies, waits for them, and re-layouts  14.5 us (6%)
  starting transfers between devices  11.5 us (5%)
  waiting for transfers between devices  5.74 us (2%)
    pallas_call x1, Pallas kernels, body(): pl.pallas_call(forward_kernel, out_shape=(shape((CHANNELS, 512, 512)), sh...  82.4 us
    pallas_call x1, Pallas kernels, body(): pl.pallas_call(adjoint_kernel, out_shape=shape((SOURCES, 8, LANES)), in_s...  79.9 us
    all_to_all x2, blocking collectives, exchange(): lax.all_to_all(message, AXES, split_axis=0, concat_axis=0, tiled=True)  34.2 us
    all_to_all x1, starting transfers between devices, exchange(): lax.all_to_all(message, AXES, split_axis=0, concat_axis=0, tiled=True)  11.5 us
    pallas_call x1, Pallas kernels, body(): pl.pallas_call(slot_kernel, out_shape=(slot, slot, slot, slot, shape((CHA...  9.49 us
    unnamed x3, local copies, waits for them, and re-layouts  7.24 us
    transpose x1, local copies, waits for them, and re-layouts, body(): beam_weights.reshape(CHANNELS, WIDTH, ROWS, BUCKETS).transpose(0, 3, 1, 2)  7.22 us
    all_to_all x1, waiting for transfers between devices, exchange(): lax.all_to_all(message, AXES, split_axis=0, concat_axis=0, tiled=True)  5.74 us
  transfers between devices with their start and end apart: 1, of which 1 were waited for; matrix products, arithmetic and copies ran while one was open for 6% of the time, Pallas kernels for 0%

profile of v1, /device:TPU:1, one launch (start us, length us, event | category | flops | bytes accessed | tf_op | source)
XLA Modules:
  0.0 242.0 jit_solution(12813961006576785677)
XLA Ops:
  0.0 2.4 %shard_map.82 = (f32[128,16,128]{2,1,0:T(8,128)}, s32[4,128]{1,0:T(4,128)}) custom-call(f32[8,128]{1,0:T(8,128)} %bitcast.10, f32[2,128]{1,0:T(2,128)} %gain_ref.1, s32[4,128]{1,0:T(4,128)} %bitcast.12, s32[4,128]{1,0:T(4,128)} %cell_ref.1), custom_call_target="tpu_custom_call" | custom-call | tf_op jit(solution)/shard_map/pallas_call | solution.py:474
  2.4 11.5 %all-to-all-start = ((f32[128,16,128]{2,1,0:T(8,128)}), f32[128,16,128]{2,1,0:T(8,128)S(1)}, u32[]{:S(2)}, u32[]{:S(2)}) async-start(f32[128,16,128]{2,1,0:T(8,128)} %get-tuple-element.15), calls=%async_computation | async-start | bytes 2097152 | tf_op jit(solution)/shard_map/all_to_all | solution.py:456
  13.9 6.3 %copy.10 = f32[4,32,4096]{1,2,0:T(8,128)} copy(f32[4,32,4096]{2,1,0:T(8,128)} %param.12) | data formatting | bytes 4194304 | tf_op args[4]
  20.2 7.2 %copy.11 = f32[4,16,32,256]{3,2,1,0:T(8,128)} copy(f32[4,16,32,256]{2,1,3,0:T(8,128)} %bitcast.7) | data formatting | bytes 4194304 | tf_op jit(solution)/shard_map/transpose | solution.py:481
  27.4 5.7 %all-to-all-done.got_ref = f32[128,16,128]{2,1,0:T(8,128)S(1)} async-done(((f32[128,16,128]{2,1,0:T(8,128)}), f32[128,16,128]{2,1,0:T(8,128)S(1)}, u32[]{:S(2)}, u32[]{:S(2)}) %all-to-all-start) | async-done | bytes 1048608 | tf_op jit(solution)/shard_map/all_to_all | solution.py:456
  33.1 0.0 copy-start
  33.2 1.0 copy-done
  34.1 9.5 %shard_map.83 = (f32[1536,128]{1,0:T(8,128)}, f32[1536,128]{1,0:T(8,128)}, f32[1536,128]{1,0:T(8,128)}, f32[1536,128]{1,0:T(8,128)}, s32[4,128,128]{2,1,0:T(8,128)}, /*index=5*/s32[8,128]{1,0:T(8,128)}) custom-call(f32[128,16,128]{2,1,0:T(8,128)} %copy-done), custom_call_target="tpu_custom_call" | custom-call | tf_op jit(solution)/shard_map/pallas_call | solution.py:484
  43.6 82.4 %shard_map.84 = (f32[4,512,512]{2,1,0:T(8,128)}, f32[128,1,128]{2,1,0:T(1,128)}) custom-call(s32[8,128]{1,0:T(8,128)} %get-tuple-element.16.most_ref, s32[1]{0:T(128)} %bitcast.2.first_ref, f32[1536,128]{1,0:T(8,128)} %get-tuple-element.17.vr_ref, f32[1536,128]{1,0:T(8,128)} %get-tuple-element.18.vi_ref, f32[1536,128]{1,0:T(8,128)} %get-tuple-element.19.row_ref, ...), custom_call_target="tpu_custom_call" | custom-call | tf_op jit(solution)/shard_map/pallas_call | solution.py:503
  126.1 15.0 %all_to_all.15.sums_ref = f32[128,1,128]{2,1,0:T(1,128)} all-to-all(f32[128,1,128]{2,1,0:T(1,128)} %get-tuple-element.21), channel_id=1, replica_groups=mesh['row'=16,'col'=8] {'row','col'}, dimensions={0} | all-to-all | bytes 131072 | tf_op jit(solution)/shard_map/all_to_all | solution.py:456
  141.0 79.9 %shard_map.85 = f32[128,8,128]{2,1,0:T(8,128)} custom-call(s32[8,128]{1,0:T(8,128)} %get-tuple-element.16.most_ref, s32[1]{0:T(128)} %bitcast.2.first_ref, f32[128,1,128]{2,1,0:T(1,128)} %all_to_all.15.sums_ref, f32[1536,128]{1,0:T(8,128)} %get-tuple-element.19.row_ref, f32[1536,128]{1,0:T(8,128)} %get-tuple-element.20.col_ref, ...), custom_call_target="tpu_custom_call" | custom-call | tf_op jit(solution)/shard_map/pallas_call | solution.py:515
  221.0 19.2 %all_to_all.16.got_ref = f32[128,8,128]{2,1,0:T(8,128)} all-to-all(f32[128,8,128]{2,1,0:T(8,128)} %shard_map.85), channel_id=1, replica_groups=mesh['row'=16,'col'=8] {'row','col'}, dimensions={0} | all-to-all | bytes 1048576 | tf_op jit(solution)/shard_map/all_to_all | solution.py:456
  240.2 1.8 shard_map.86
Async XLA Ops:
  2.4 30.7 %all-to-all-start = ((f32[128,16,128]{2,1,0:T(8,128)}), f32[128,16,128]{2,1,0:T(8,128)S(1)}, u32[]{:S(2)}, u32[]{:S(2)}) async-start(f32[128,16,128]{2,1,0:T(8,128)} %get-tuple-element.15), calls=%async_computation | async-start | bytes 2097152 | tf_op jit(solution)/shard_map/all_to_all | solution.py:456
  33.1 1.0 copy-start
